TPU v7x, 256 devices: a whole 4x4x8 slice. The times are simulated.
256 devices in a mesh: ctx: 32 (over y, z), head: 8 (over x, core).
Axes of the slice: x: 4, y: 4, z: 8, core: 2. Of those that a mesh axis runs over, the one named last changes fastest.
Arguments:
- queries: bfloat16 [8192, 4096], P('ctx', 'head'), may hold values from -6 to 6
- key_rows: bfloat16 [8192, 4096], P('ctx', 'head'), may hold values from -0.5 to 0.5
- value_rows: bfloat16 [8192, 4096], P('ctx', 'head'), may hold values from -6 to 6
- doc_ids: int32 [8192], P('ctx'), may hold values from 0 to 15, never falling along the last dimension, each value on 1 to 2048 neighbouring positions
- out_grad: bfloat16 [8192, 6144], P(('ctx', 'head')), may hold values from -6 to 6
- out_weight: bfloat16 [4096, 6144], P('head', 'ctx'), may hold values from -0.09375 to 0.09375
Outputs:
- layer_out: bfloat16 [8192, 6144], P(('ctx', 'head'))
- query_grad: bfloat16 [8192, 4096], P('ctx', 'head')
- key_grad: bfloat16 [8192, 4096], P('ctx', 'head')
- value_grad: bfloat16 [8192, 4096], P('ctx', 'head')
- weight_grad: bfloat16 [4096, 6144], P(('head', 'ctx'))
Inputs may be any that keep to these rules, and one draw needn't show every extreme that they name: `doc_ids`: repository ids never fall along the sequence; each repository covers 1 to 2048 tokens, and one covers exactly that many.
All inputs are finite; a program needn't handle non-finite values.
Results may differ from a plain program's by a relative error of at most 0.025.
Values may be sent and summed in bfloat16 or wider, within the bound.
No kernel may reach another device: no remote copies, remote signals or barrier semaphores. Data moves between devices by JAX's collectives and lax.ppermute only.
A program may use at most 128 MiB of HBM per device.

v0:
```python
import jax
import jax.numpy as jnp
from jax import lax
from jax.sharding import PartitionSpec as P

HD = 128
EPSILON = 1e-05


def carried_in(x, axis, join, neutral, backward):
    count = lax.axis_size(axis)
    place = lax.axis_index(axis)
    ahead = count - 1 - place if backward else place
    gathered = jax.tree.map(
        lambda a, kind: lax.all_gather(a.astype(kind), axis),
        x,
        (jnp.bfloat16, jnp.bfloat16, jnp.bfloat16),
    )
    state = jax.tree.map(lambda a, e: jnp.zeros_like(a) + jnp.asarray(e, a.dtype), x, neutral)

    def one(lap, state):
        source = count - 1 - lap if backward else lap
        return join(
            state,
            jax.tree.map(
                lambda a, own: lax.dynamic_index_in_dim(a, source, 0, False).astype(own.dtype),
                gathered,
                x,
            ),
        )

    return lax.fori_loop(0, ahead, one, state)


def forward_link(earlier_part, later_part):
    early_first, early_last, early_state = earlier_part
    late_first, late_last, late_state = later_part
    late_empty = late_last < 0.0
    early_empty = early_last < 0.0
    linked = (early_last == late_first) & (late_first == late_last)
    joined = late_state + jnp.where(linked, early_state, jnp.float32(0.0))
    return (
        jnp.where(early_empty, late_first, early_first),
        jnp.where(late_empty, early_last, late_last),
        jnp.where(late_empty, early_state, joined),
    )


def backward_link(earlier_part, later_part):
    high_first, high_last, high_state = earlier_part
    low_first, low_last, low_state = later_part
    low_empty = low_last < 0.0
    high_empty = high_last < 0.0
    linked = (high_first == low_last) & (low_first == low_last)
    joined = low_state + jnp.where(linked, high_state, jnp.float32(0.0))
    return (
        jnp.where(low_empty, high_first, low_first),
        jnp.where(high_empty, low_last, high_last),
        jnp.where(low_empty, high_state, joined),
    )


def shards(queries, key_rows, value_rows, doc_ids, out_grad, out_weight):
    tok_count, full_width = queries.shape
    head_count = full_width // HD
    query_heads = queries.reshape(tok_count, head_count, HD)
    key_heads = key_rows.reshape(tok_count, head_count, HD)
    value_heads = value_rows.reshape(tok_count, head_count, HD)
    doc_values = doc_ids.astype(jnp.float32)
    first_doc = doc_values[:1]
    last_doc = doc_values[-1:]
    causal = jnp.tril(jnp.ones((tok_count, tok_count), dtype=bool))
    allowed = (causal & (doc_ids[:, None] == doc_ids[None, :]))[None]
    scores = jnp.einsum("thd,shd->hts", query_heads, key_heads, preferred_element_type=jnp.float32)
    weights = jnp.where(allowed, scores, jnp.float32(0.0)).astype(jnp.bfloat16)
    key_last = jnp.where(
        (doc_values == last_doc)[:, None, None], key_heads, jnp.zeros_like(key_heads)
    )
    local_state = jnp.einsum(
        "thd,the->hde", key_last, value_heads, preferred_element_type=jnp.float32
    )
    empty_marks = jnp.full((1,), -1.0, jnp.float32)
    identity = (empty_marks, empty_marks, jnp.zeros_like(local_state))
    prior_first, prior_last, prior_state = carried_in(
        (first_doc, last_doc, local_state), "ctx", forward_link, identity, False
    )
    row_mask = doc_values == prior_last
    prior_rounded = prior_state.astype(jnp.bfloat16)
    inter = jnp.einsum(
        "thd,hde->the", query_heads, prior_rounded, preferred_element_type=jnp.float32
    )
    mixed = jnp.einsum(
        "hts,she->the", weights, value_heads, preferred_element_type=jnp.float32
    ) + jnp.where(row_mask[:, None, None], inter, jnp.float32(0.0))
    inv_norm = lax.rsqrt(jnp.mean(mixed * mixed, axis=-1, keepdims=True) + EPSILON)
    normed = mixed * inv_norm
    normed_flat = normed.astype(jnp.bfloat16).reshape(tok_count, full_width)
    full_weight = lax.all_gather(out_weight, "ctx", axis=1, tiled=True)
    layer_out = lax.psum_scatter(
        jnp.dot(normed_flat, full_weight, preferred_element_type=jnp.float32).astype(jnp.bfloat16),
        "head",
        scatter_dimension=0,
        tiled=True,
    )
    grad_full = lax.all_gather(out_grad, "head", axis=0, tiled=True)
    grad_normed = lax.dot_general(
        grad_full, full_weight, (((1,), (1,)), ((), ())), preferred_element_type=jnp.float32
    ).reshape(tok_count, head_count, HD)
    mixed_grad = (
        inv_norm * (grad_normed - normed * jnp.mean(grad_normed * normed, axis=-1, keepdims=True))
    ).astype(jnp.bfloat16)
    weight_grad = lax.psum_scatter(
        lax.dot_general(
            normed_flat, grad_full, (((0,), (0,)), ((), ())), preferred_element_type=jnp.float32
        ).astype(jnp.bfloat16),
        "ctx",
        scatter_dimension=0,
        tiled=True,
    )
    query_first = jnp.where(
        (doc_values == first_doc)[:, None, None], query_heads, jnp.zeros_like(query_heads)
    )
    local_future = jnp.einsum(
        "thd,the->hde", query_first, mixed_grad, preferred_element_type=jnp.float32
    )
    later_first, later_last, future_state = carried_in(
        (first_doc, last_doc, local_future), "ctx", backward_link, identity, True
    )
    col_mask = (doc_values == later_first)[:, None, None]
    future_rounded = future_state.astype(jnp.bfloat16)
    grad_raw = jnp.einsum(
        "the,she->hts", mixed_grad, value_heads, preferred_element_type=jnp.float32
    )
    grad_scores = jnp.where(allowed, grad_raw, jnp.float32(0.0)).astype(jnp.bfloat16)
    query_grad = jnp.einsum(
        "hts,shd->thd", grad_scores, key_heads, preferred_element_type=jnp.float32
    ) + jnp.where(
        row_mask[:, None, None],
        jnp.einsum("the,hde->thd", mixed_grad, prior_rounded, preferred_element_type=jnp.float32),
        jnp.float32(0.0),
    )
    key_grad = jnp.einsum(
        "hts,thd->shd", grad_scores, query_heads, preferred_element_type=jnp.float32
    ) + jnp.where(
        col_mask,
        jnp.einsum("she,hde->shd", value_heads, future_rounded, preferred_element_type=jnp.float32),
        jnp.float32(0.0),
    )
    value_grad = jnp.einsum(
        "hts,the->she", weights, mixed_grad, preferred_element_type=jnp.float32
    ) + jnp.where(
        col_mask,
        jnp.einsum("shd,hde->she", key_heads, future_rounded, preferred_element_type=jnp.float32),
        jnp.float32(0.0),
    )
    return (
        layer_out,
        query_grad.astype(jnp.bfloat16).reshape(tok_count, full_width),
        key_grad.astype(jnp.bfloat16).reshape(tok_count, full_width),
        value_grad.astype(jnp.bfloat16).reshape(tok_count, full_width),
        weight_grad,
    )


def solution(mesh):
    return jax.shard_map(
        shards,
        mesh=mesh,
        in_specs=(
            P("ctx", "head"),
            P("ctx", "head"),
            P("ctx", "head"),
            P("ctx"),
            P(("ctx", "head"), None),
            P("head", "ctx"),
        ),
        out_specs=(
            P(("ctx", "head"), None),
            P("ctx", "head"),
            P("ctx", "head"),
            P("ctx", "head"),
            P(("head", "ctx"), None),
        ),
        check_vma=False,
    )
```

profile of v0, /device:TPU:2, one launch (start us, length us, event | category | flops | bytes accessed | tf_op | source)
XLA Modules:
  0.0 609.2 jit_solution(14436302235198908007)
XLA Ops:
  7.9 1.1 copy.86
  9.6 2.0 broadcast_compare_fusion.1
  14.0 1.3 dynamic-slice
  15.9 1.4 dynamic-update-slice
  17.3 1.4 dynamic-update-slice.1
  18.7 78.3 %all-reduce.2 = (bf16[32]{0:T(256)(128)(2,1)S(1)}, bf16[32]{0:T(256)(128)(2,1)S(1)}) all-reduce(bf16[32]{0:T(256)(128)(2,1)S(1)} %dynamic-update-slice, bf16[32]{0:T(256)(128)(2,1)S(1)} %dynamic-update-slice.1), channel_id=2, replica_groups=mesh['ctx'=32,'head'=8] {'ctx'}, use_global_device_ids=true, to_apply=%add | all-reduce | flops 64 | bytes 256
  97.0 1.1 copy.59
  99.0 1.3 fusion.2
  101.0 24.8 %all-gather.11.cloned.1.call-done = bf16[256,6144]{1,0:T(8,128)(2,1)} async-done(((bf16[32,6144]{1,0:T(8,128)(2,1)}), bf16[256,6144]{1,0:T(8,128)(2,1)}) %all-gather.11.cloned.1.call-update) | async-done | bytes 3145744 | tf_op jit(solution)/shard_map/all_gather | solution.py:105
  125.8 92.5 %all-gather.9.cloned.1.call-done = bf16[512,6144]{0,1:T(8,128)(2,1)} async-done(((bf16[512,192]{0,1:T(8,128)(2,1)}), bf16[512,6144]{0,1:T(8,128)(2,1)}) %all-gather.9.cloned.1.call-update) | async-done | bytes 6291472 | tf_op jit(solution)/shard_map/all_gather | solution.py:98
  218.2 6.3 %multiply_reduce_fusion = (f32[256,4]{0,1:T(4,128)S(1)}, f32[256,512]{0,1:T(8,128)S(1)}) fusion(f32[256,4,128]{0,2,1:T(8,128)S(1)} %get-tuple-element.234, f32[256,4]{0,1:T(4,128)S(1)} %add_rsqrt_fusion, bf16[256,6144]{1,0:T(8,128)(2,1)} %all-gather.11.cloned.1.call-done, bf16[512,6144]{0,1:T(8,128)(2,1)} %all-gather.9.cloned.1.call-done), kind=kOutput, calls=%fused_computation.34 | convolution fusion | flops 1611004928 | bytes 10493952 | tf_op jit(solution)/shard_map/dot_general | solution.py:106
  224.7 0.9 convolution_convert_fusion.2
  225.6 6.4 %convolution_convert_fusion.1 = bf16[256,6144]{1,0:T(8,128)(2,1)} fusion(bf16[256,512]{0,1:T(8,128)(2,1)S(1)} %bitcast.132, bf16[512,6144]{0,1:T(8,128)(2,1)} %all-gather.9.cloned.1.call-done), kind=kOutput, calls=%fused_computation.9 | convolution fusion | flops 1612185600 | bytes 9699328 | tf_op jit(solution)/shard_map/dot_general | solution.py:100
  232.1 6.4 %convolution_convert_fusion = bf16[512,6144]{1,0:T(8,128)(2,1)} fusion(bf16[256,512]{0,1:T(8,128)(2,1)S(1)} %bitcast.133, bf16[256,6144]{1,0:T(8,128)(2,1)} %all-gather.11.cloned.1.call-done), kind=kOutput, calls=%fused_computation.8 | convolution fusion | flops 1613758464 | bytes 9699328 | tf_op jit(solution)/shard_map/dot_general | solution.py:113
  240.7 94.9 %all-gather.15.cloned.1.call-done = bf16[128,128,128]{2,1,0:T(8,128)(2,1)} async-done(((bf16[4,128,128]{2,1,0:T(8,128)(2,1)}), bf16[128,128,128]{2,1,0:T(8,128)(2,1)}) %all-gather.15.cloned.1.call-update) | async-done | bytes 4194320 | tf_op jit(solution)/shard_map/all_gather | solution.py:15
  335.7 158.6 %while.31 = (s32[]{:T(128)}, f32[1]{0:T(128)}, f32[4,128,128]{2,1,0:T(8,128)S(1)}, s32[]{:T(128)}, bf16[32,1]{0,1:T(2,128)(2,1)S(1)}, /*index=5*/bf16[32,1]{0,1:...) while((s32[]{:T(128)}, f32[1]{0:T(128)}, ...), condition=%wide.region_6.7_spmd, body=%wide.region_5.6_spmd.sunk | while | flops 262155 | bytes 655590 | solution.py:32
  339.7 1.0 fusion.69
  344.8 1.0 fusion.69
  350.0 1.0 fusion.69
  355.1 1.0 fusion.69
  360.2 1.0 fusion.69
  365.3 1.0 fusion.69
  370.4 1.0 fusion.69
  375.5 1.0 fusion.69
  380.7 1.0 fusion.69
  385.8 1.0 fusion.69
  390.9 1.0 fusion.69
  396.0 1.0 fusion.69
  401.1 1.0 fusion.69
  406.2 1.0 fusion.69
  411.3 1.0 fusion.69
  416.5 1.0 fusion.69
  421.6 1.0 fusion.69
  426.7 1.0 fusion.69
  431.8 1.0 fusion.69
  436.9 1.0 fusion.69
  442.0 1.1 fusion.69
  447.2 1.0 fusion.69
  452.3 1.0 fusion.69
  457.4 1.0 fusion.69
  462.5 1.0 fusion.69
  467.6 1.0 fusion.69
  472.7 1.0 fusion.69
  477.9 1.0 fusion.69
  483.0 1.0 fusion.69
  488.1 1.0 fusion.69
  493.2 1.0 fusion.69
  496.5 105.9 %reduce-scatter.5.cloned.1.call-done = bf16[16,6144]{1,0:T(8,128)(2,1)} async-done(((bf16[512,6144]{1,0:T(8,128)(2,1)}), bf16[16,6144]{1,0:T(8,128)(2,1)}) %reduce-scatter.5.cloned.1.call-update) | async-done | bytes 196624 | tf_op jit(solution)/shard_map/reduce_scatter | solution.py:112
  (78 shorter events, 31.2 us)
Async XLA Ops:
  7.2 4.4 copy-start
  7.2 93.4 %all-gather.13.cloned.1.call-start = ((), (), s32[]{:S(2)}) async-start(), calls=%async_computation.6 | async-start | bytes 4325376 | tf_op jit(solution)/shard_map/all_gather | solution.py:15
  11.6 89.1 %copy-start.2 = (s32[256]{0:T(256)S(1)}, s32[256]{0:T(256)}, u32[]{:S(2)}) copy-start(s32[256]{0:T(256)} %param.13) | copy-start | bytes 3076
  12.5 113.3 %all-gather.11.cloned.1.call-start = ((), (), s32[]{:S(2)}) async-start(), calls=%async_computation.4 | async-start | bytes 3538944 | tf_op jit(solution)/shard_map/all_gather | solution.py:105
  13.2 205.0 %all-gather.9.cloned.1.call-start = ((), (), s32[]{:S(2)}) async-start(), calls=%async_computation.2 | async-start | bytes 6488064 | tf_op jit(solution)/shard_map/all_gather | solution.py:98
  14.0 321.7 %all-gather.15.cloned.1.call-start = ((), (), s32[]{:S(2)}) async-start(), calls=%async_computation.7 | async-start | bytes 4325376 | tf_op jit(solution)/shard_map/all_gather | solution.py:15
  225.6 270.9 %reduce-scatter.3.cloned.1.call-start = ((), (), s32[]{:S(2)}) async-start(), calls=%async_computation.3 | async-start | bytes 3538944 | tf_op jit(solution)/shard_map/reduce_scatter | solution.py:99
  232.1 370.3 %reduce-scatter.5.cloned.1.call-start = ((), (), s32[]{:S(2)}) async-start(), calls=%async_computation.5 | async-start | bytes 6488064 | tf_op jit(solution)/shard_map/reduce_scatter | solution.py:112
  240.2 255.1 %copy-start.1 = (bf16[256,512]{1,0:T(8,128)(2,1)S(1)}, bf16[256,512]{1,0:T(8,128)(2,1)}, u32[]{:S(2)}) copy-start(bf16[256,512]{1,0:T(8,128)(2,1)} %param.11) | copy-start | bytes 786436
Sparse Core Ops, SparseCore 0:
  12.6 84.7 all-gather.12
  99.3 26.4 all-gather.10
  128.3 89.8 all-gather.8
  225.7 109.8 all-gather.14
  338.6 32.1 reduce-scatter.2
  375.2 227.1 reduce-scatter.4
where the time goes:
time: 612 us; the launch traced here: 609 us
  waiting for transfers between devices  320 us (52%)
  loops' own time  105 us (17%)
  blocking collectives  78.3 us (13%)
  other arithmetic  36.1 us (6%)
  local copies, waits for them, and re-layouts  30.8 us (5%)
  matrix products  24.5 us (4%)
  between operations  14.3 us (2%)
    reduce_scatter x1, waiting for transfers between devices, shards(): lax.psum_scatter(lax.dot_general(normed_flat, grad_full, (((0,), (0,)), (...  106 us
    another operation x2, loops' own time, carried_in(): return lax.fori_loop(0, ahead, one, state)  105 us
    all_gather x2, waiting for transfers between devices, carried_in(): lax.all_gather(a.astype(kind), axis)  95 us
    all_gather x1, waiting for transfers between devices, shards(): full_weight = lax.all_gather(out_weight, 'ctx', axis=1, tiled=True)  92.5 us
    unnamed x1, blocking collectives  78.3 us
    select_n x31, other arithmetic, backward_link(): jnp.where(low_empty, high_state, joined)  32.4 us
    all_gather x1, waiting for transfers between devices, shards(): grad_full = lax.all_gather(out_grad, 'head', axis=0, tiled=True)  24.8 us
    dynamic_slice x31, local copies, waits for them, and re-layouts, one(): lax.dynamic_index_in_dim(a, source, 0, False).astype(own.dtype)  20.8 us
  transfers between devices with their start and end apart: 6, of which 4 were waited for; matrix products, arithmetic and copies ran while one was open for 13% of the time, Pallas kernels for 0%

commit v1 on v0

--- a/solution.py
+++ b/solution.py
@@ -95,7 +95,9 @@
     inv_norm = lax.rsqrt(jnp.mean(mixed * mixed, axis=-1, keepdims=True) + EPSILON)
     normed = mixed * inv_norm
     normed_flat = normed.astype(jnp.bfloat16).reshape(tok_count, full_width)
-    full_weight = lax.all_gather(out_weight, "ctx", axis=1, tiled=True)
+    full_weight = jnp.concatenate(
+        lax.all_to_all(jnp.stack([out_weight] * lax.axis_size("ctx")), "ctx", 0, 0), axis=1
+    )
     layer_out = lax.psum_scatter(
         jnp.dot(normed_flat, full_weight, preferred_element_type=jnp.float32).astype(jnp.bfloat16),
         "head",

time: 612 us -> 779 us (1.27)
  blocking collectives: 78.3 us -> 224 us
  starting transfers between devices: 0.24 us -> 11.9 us
  local copies, waits for them, and re-layouts: 30.8 us -> 41.4 us
    unnamed x1, blocking collectives: 78.3 us -> 224 us
    all_gather x2, waiting for transfers between devices: 95 us -> 212 us  [carried_in(): lax.all_gather(a.astype(kind), axis)]
    all_gather x1 -> x0, waiting for transfers between devices: 92.5 us -> none  [shards(): full_weight = lax.all_gather(out_weight, 'ctx', axis=1, tiled=True)]
    all_gather x1, waiting for transfers between devices: 24.8 us -> 0.01 us  [shards(): grad_full = lax.all_gather(out_grad, 'head', axis=0, tiled=True)]
    all_to_all x0 -> x1, starting transfers between devices: none -> 11.7 us  [shards(): lax.all_to_all(jnp.stack([out_weight] * lax.axis_size('ctx')), 'ctx', 0, 0)]
    dot_general x0 -> x1, local copies, waits for them, and re-layouts: none -> 9.75 us  [shards(): lax.dot_general(grad_full, full_weight, (((1,), (1,)), ((), ())), preferr...]
  transfers between devices with their start and end apart: 6 -> 6, of which waited for: 4 -> 2; matrix products, arithmetic and copies ran while one was open for 13% -> 11% of each run, Pallas kernels for 0% -> 0%
where the time goes in v1:
time: 779 us; the launch traced here: 777 us
  waiting for transfers between devices  326 us (42%)
  blocking collectives  224 us (29%)
  loops' own time  101 us (13%)
  local copies, waits for them, and re-layouts  41.4 us (5%)
  other arithmetic  35.3 us (5%)
  matrix products  23.6 us (3%)
  between operations  14 us (2%)
  starting transfers between devices  11.9 us (2%)
    unnamed x1, blocking collectives  224 us
    all_gather x2, waiting for transfers between devices, carried_in(): lax.all_gather(a.astype(kind), axis)  212 us
    reduce_scatter x1, waiting for transfers between devices, shards(): lax.psum_scatter(lax.dot_general(normed_flat, grad_full, (((0,), (0,)), (...  112 us
    another operation x2, loops' own time, carried_in(): return lax.fori_loop(0, ahead, one, state)  101 us
    select_n x31, other arithmetic, backward_link(): jnp.where(low_empty, high_state, joined)  32.4 us
    dynamic_slice x31, local copies, waits for them, and re-layouts, one(): lax.dynamic_index_in_dim(a, source, 0, False).astype(own.dtype)  19 us
  transfers between devices with their start and end apart: 6, of which 2 were waited for; matrix products, arithmetic and copies ran while one was open for 11% of the time, Pallas kernels for 0%

profile of v1, /device:TPU:2, one launch (start us, length us, event | category | flops | bytes accessed | tf_op | source)
XLA Modules:
  0.0 776.9 jit_solution(12155005538287813001)
XLA Ops:
  8.5 1.1 copy.108
  9.6 2.0 broadcast_compare_fusion.1
  11.6 0.9 convolution_convert_fusion.3
  12.5 4.3 stack.2
  16.8 11.7 %all-to-all-start = ((bf16[32,512,192]{1,2,0:T(8,128)(2,1)}), bf16[32,512,192]{1,2,0:T(8,128)(2,1)}, u32[]{:S(2)}, u32[]{:S(2)}) async-start(bf16[32,512,192]{1,2,0:T(8,128)(2,1)} %stack.2), calls=%async_computation | async-start | bytes 12582912 | tf_op jit(solution)/shard_map/all_to_all | solution.py:99
  30.5 1.4 dynamic-update-slice
  31.9 1.4 dynamic-update-slice.1
  33.3 224.4 %all-reduce.2 = (bf16[32]{0:T(256)(128)(2,1)S(1)}, bf16[32]{0:T(256)(128)(2,1)S(1)}) all-reduce(bf16[32]{0:T(256)(128)(2,1)S(1)} %dynamic-update-slice, bf16[32]{0:T(256)(128)(2,1)S(1)} %dynamic-update-slice.1), channel_id=2, replica_groups=mesh['ctx'=32,'head'=8] {'ctx'}, use_global_device_ids=true, to_apply=%add | all-reduce | flops 64 | bytes 256
  259.1 9.8 %dot_general.52 = bf16[4,128,6144]{1,0,2:T(4,128)(2,1)} reshape(bf16[512,32,192]{0,2,1:T(8,128)(2,1)} %bitcast.23) | data formatting | bytes 12582912 | tf_op jit(solution)/shard_map/dot_general | solution.py:108
  268.8 6.3 multiply_reduce_fusion
  275.2 0.9 convolution_convert_fusion.2
  276.2 6.4 convolution_convert_fusion.1
  282.7 6.4 convolution_convert_fusion
  290.0 0.8 copy.71
  291.3 212.5 %all-gather.12.cloned.1.call-done = bf16[128,128,128]{2,1,0:T(8,128)(2,1)} async-done(((bf16[4,128,128]{2,1,0:T(8,128)(2,1)}), bf16[128,128,128]{2,1,0:T(8,128)(2,1)}) %all-gather.12.cloned.1.call-update) | async-done | bytes 4194320 | tf_op jit(solution)/shard_map/all_gather | solution.py:15
  503.8 152.1 %while.31 = (s32[]{:T(128)}, f32[1]{0:T(128)}, f32[4,128,128]{2,1,0:T(8,128)S(1)}, s32[]{:T(128)}, bf16[32,1]{0,1:T(2,128)(2,1)S(1)}, /*index=5*/bf16[32,1]{0,1:...) while((s32[]{:T(128)}, f32[1]{0:T(128)}, ...), condition=%wide.region_6.7_spmd, body=%wide.region_5.6_spmd.sunk | while | flops 262155 | bytes 655574 | solution.py:32
  507.0 1.0 fusion.70
  511.9 1.0 fusion.70
  516.8 1.0 fusion.70
  521.7 1.0 fusion.70
  526.6 1.0 fusion.70
  531.5 1.0 fusion.70
  536.4 1.0 fusion.70
  541.3 1.0 fusion.70
  546.2 1.0 fusion.70
  551.1 1.0 fusion.70
  556.0 1.0 fusion.70
  560.9 1.0 fusion.70
  565.8 1.0 fusion.70
  570.8 1.0 fusion.70
  575.7 1.0 fusion.70
  580.6 1.0 fusion.70
  585.5 1.0 fusion.70
  590.4 1.0 fusion.70
  595.3 1.0 fusion.70
  600.2 1.0 fusion.70
  605.1 1.0 fusion.70
  610.0 1.0 fusion.70
  614.9 1.0 fusion.70
  619.8 1.0 fusion.70
  624.7 1.0 fusion.70
  629.6 1.0 fusion.70
  634.5 1.0 fusion.70
  639.4 1.0 fusion.70
  644.3 1.0 fusion.70
  649.3 1.0 fusion.70
  654.2 1.0 fusion.70
  658.1 112.3 %reduce-scatter.5.cloned.1.call-done = bf16[16,6144]{1,0:T(8,128)(2,1)} async-done(((bf16[512,6144]{1,0:T(8,128)(2,1)}), bf16[16,6144]{1,0:T(8,128)(2,1)}) %reduce-scatter.5.cloned.1.call-update) | async-done | bytes 196624 | tf_op jit(solution)/shard_map/reduce_scatter | solution.py:114
  (83 shorter events, 27.3 us)
Async XLA Ops:
  7.2 4.4 copy-start
  7.2 251.5 %all-gather.10.cloned.1.call-start = ((), (), s32[]{:S(2)}) async-start(), calls=%async_computation.6 | async-start | bytes 4325376 | tf_op jit(solution)/shard_map/all_gather | solution.py:15
  16.7 12.6 %copy-start.4 = (u32[256]{0:T(256)S(1)}, u32[256]{0:T(256)}, u32[]{:S(2)}) copy-start(u32[256]{0:T(256)} %constant.98) | copy-start | bytes 3076
  16.8 241.0 %copy-start.2 = (bf16[256,512]{1,0:T(8,128)(2,1)S(1)}, bf16[256,512]{1,0:T(8,128)(2,1)}, u32[]{:S(2)}) copy-start(bf16[256,512]{1,0:T(8,128)(2,1)} %param.10) | copy-start | bytes 786436
  16.8 241.1 %copy-start.3 = (s32[256]{0:T(256)S(1)}, s32[256]{0:T(256)}, u32[]{:S(2)}) copy-start(s32[256]{0:T(256)} %param.13) | copy-start | bytes 3076
  16.8 241.2 %copy-start.1 = (bf16[256,512]{1,0:T(8,128)(2,1)S(1)}, bf16[256,512]{1,0:T(8,128)(2,1)}, u32[]{:S(2)}) copy-start(bf16[256,512]{1,0:T(8,128)(2,1)} %param.11) | copy-start | bytes 786436
  16.8 242.3 %all-to-all-start = ((bf16[32,512,192]{1,2,0:T(8,128)(2,1)}), bf16[32,512,192]{1,2,0:T(8,128)(2,1)}, u32[]{:S(2)}, u32[]{:S(2)}) async-start(bf16[32,512,192]{1,2,0:T(8,128)(2,1)} %stack.2), calls=%async_computation | async-start | bytes 12582912 | tf_op jit(solution)/shard_map/all_to_all | solution.py:99
  28.5 240.3 %all-gather.8.cloned.1.call-start = ((), (), s32[]{:S(2)}) async-start(), calls=%async_computation.4 | async-start | bytes 3538944 | tf_op jit(solution)/shard_map/all_gather | solution.py:107
  29.3 474.5 %all-gather.12.cloned.1.call-start = ((), (), s32[]{:S(2)}) async-start(), calls=%async_computation.7 | async-start | bytes 4325376 | tf_op jit(solution)/shard_map/all_gather | solution.py:15
  276.2 381.9 %reduce-scatter.3.cloned.1.call-start = ((), (), s32[]{:S(2)}) async-start(), calls=%async_computation.3 | async-start | bytes 3538944 | tf_op jit(solution)/shard_map/reduce_scatter | solution.py:101
  282.7 487.7 %reduce-scatter.5.cloned.1.call-start = ((), (), s32[]{:S(2)}) async-start(), calls=%async_computation.5 | async-start | bytes 6488064 | tf_op jit(solution)/shard_map/reduce_scatter | solution.py:114
Sparse Core Ops, SparseCore 0:
  12.6 136.4 all-gather.9
  150.9 37.8 all-gather.7
  276.3 227.4 all-gather.11
  506.7 32.1 reduce-scatter.2
  543.4 226.9 reduce-scatter.4
